TPU v7x, 128 devices: a whole 4x4x4 slice. The times are simulated.
128 devices in a mesh: ctx: 16 (over y, z_lo, core), dp: 8 (over z_hi, x).
Axes of the slice: x: 4, y: 4, z: 4 (z_hi: 2, z_lo: 2; z = z_hi * 2 + z_lo), core: 2. Of those that a mesh axis runs over, the one named last changes fastest.
Arguments:
- query_rows: bfloat16 [8, 2048, 1024], P('dp', 'ctx'), may hold values from -6 to 6
- key_rows: bfloat16 [8, 2048, 1024], P('dp', 'ctx'), may hold values from -6 to 6
- value_rows: bfloat16 [8, 2048, 1024], P('dp', 'ctx'), may hold values from -6 to 6
- block_lists: int32 [8, 16, 4], P('dp'), may hold values from 0 to 15, as said below
- block_lengths: int32 [8, 16], P('dp'), may hold values from 2 to 128, as said below
- out_weight: bfloat16 [1024, 2048], replicated, may hold values from -0.125 to 0.125
- expert_input: bfloat16 [8, 2048, 2048], P('dp', 'ctx'), may hold values from -6 to 6
- layer_grad: bfloat16 [8, 2048, 2048], P('dp', 'ctx'), may hold values from -1.5 to 1.5
- route_experts: int32 [8, 2048, 6], P('dp', 'ctx'), may hold values from 0 to 15, all different within a row; in each aligned block of 128 rows (0 to 127, 128 to 255, ..., all dimensions but the last counted through in order) at most 64 rows name the same one
- route_weight: float32 [8, 2048, 6], P('dp', 'ctx'), may hold values from 0.02 to 0.4
- gate_weight: bfloat16 [16, 2048, 704], P('ctx'), may hold values from -0.125 to 0.125
- up_weight: bfloat16 [16, 2048, 704], P('ctx'), may hold values from -0.125 to 0.125
- down_weight: bfloat16 [16, 2048, 704], P('ctx'), may hold values from -0.21875 to 0.21875
Outputs:
- query_grad: bfloat16 [8, 2048, 1024], P('dp', 'ctx')
- key_grad: bfloat16 [8, 2048, 1024], P('dp', 'ctx')
- value_grad: bfloat16 [8, 2048, 1024], P('dp', 'ctx')
- gate_grad: float32 [16, 2048, 704], P('ctx', 'dp')
- up_grad: float32 [16, 2048, 704], P('ctx', 'dp')
- down_grad: float32 [16, 2048, 704], P('ctx', 'dp')
Inputs may be any that keep to these rules, and one draw needn't show every extreme that they name: `block_lists`: entry 0 of row i of a sequence's lists is i; every entry of row i lies in 0 to i. `block_lengths`: every sequence has a block of full length 128. `route_experts`: each token names 6 different experts. Among the 128 tokens of one device, no expert is named by more than 64 tokens.
All inputs are finite; a program needn't handle non-finite values.
Results may differ from a plain program's by a relative error of at most 0.012.
The roundings to bfloat16 on the way count: a program that leaves them out, or rounds other values in their place, can miss the bound.
Values may be sent and summed in bfloat16 or wider, within the bound.
No kernel may reach another device: no remote copies, remote signals or barrier semaphores. Data moves between devices by JAX's collectives and lax.ppermute only.
A program may use at most 192 MiB of HBM per device.

v0:
```python
import math
import jax
import jax.numpy as jnp
from jax import lax
from jax.sharding import PartitionSpec as P

HEADS = 8
HD = 128
TOPK = 6
EXP_DEV = 1
BLK = 128
NSEL = 4


def route_coefficients(chosen, rweights, expert_list):
    matches = chosen[:, :, None] == expert_list[None, None, :]
    return jnp.sum(jnp.where(matches, rweights[:, :, None], 0.0), axis=1)


def slot_rows(tokens, grad_rows, coef_rows, capacity):
    present = coef_rows > 0.0
    rank_rows = jnp.cumsum(present.astype(jnp.int32), axis=0) - 1
    slot_ids = jnp.arange(capacity, dtype=jnp.int32)
    chosen_slot = present.T[:, None, :] & (rank_rows.T[:, None, :] == slot_ids[None, :, None])
    onehot = chosen_slot.astype(jnp.bfloat16)
    picked = jnp.einsum("ecs,sd->ecd", onehot, tokens, preferred_element_type=jnp.float32).astype(
        jnp.bfloat16
    )
    picked_grad = jnp.einsum("ecs,sd->ecd", onehot, grad_rows, preferred_element_type=jnp.float32)
    slot_coef = jnp.sum(jnp.where(chosen_slot, coef_rows.T[:, None, :], 0.0), axis=2)
    scaled = (slot_coef[:, :, None] * picked_grad).astype(jnp.bfloat16)
    return (picked, scaled)


def per_device(
    query_rows,
    key_rows,
    value_rows,
    block_lists,
    block_lengths,
    out_weight,
    expert_input,
    layer_grad,
    route_experts,
    route_weight,
    gate_weight,
    up_weight,
    down_weight,
):
    ctx_count = lax.axis_size("ctx")
    my_index = lax.axis_index("ctx")
    local_rows = query_rows.shape[1]
    seq_len = local_rows * ctx_count
    block_total = seq_len // BLK
    row_width = HEADS * HD
    inv_root = 1.0 / math.sqrt(HD)
    my_start = my_index * local_rows
    queries = query_rows[0]
    out_grad = jnp.einsum(
        "sd,wd->sw", layer_grad[0], out_weight, preferred_element_type=jnp.float32
    ).astype(jnp.bfloat16)
    whole_keys, whole_values = (
        lax.all_gather(key_rows[0], "ctx", axis=0, tiled=True),
        lax.all_gather(value_rows[0], "ctx", axis=0, tiled=True),
    )
    lengths_row = block_lengths[0]
    query_blocks = local_rows // BLK
    lists_here = lax.dynamic_slice_in_dim(block_lists[0], my_index * query_blocks, query_blocks, 0)
    entry_ids = jnp.arange(NSEL, dtype=jnp.int32)
    repeated = jnp.any(
        (lists_here[:, :, None] == lists_here[:, None, :])
        & (entry_ids[None, None, :] < entry_ids[None, :, None]),
        axis=2,
    )
    key_tiles = whole_keys.reshape(block_total, BLK, HEADS, HD)[lists_here].reshape(
        query_blocks, NSEL * BLK, HEADS, HD
    )
    value_tiles = whole_values.reshape(block_total, BLK, HEADS, HD)[lists_here].reshape(
        query_blocks, NSEL * BLK, HEADS, HD
    )
    offsets = jnp.arange(BLK, dtype=jnp.int32)
    key_pos = (lists_here[:, :, None] * BLK + offsets[None, None, :]).reshape(
        query_blocks, NSEL * BLK
    )
    present = (
        (offsets[None, None, :] < lengths_row[lists_here][:, :, None])
        & jnp.logical_not(repeated)[:, :, None]
    ).reshape(query_blocks, NSEL * BLK)
    query_pos = my_start + (
        jnp.arange(query_blocks, dtype=jnp.int32)[:, None] * BLK + offsets[None, :]
    )
    allowed = present[:, None, :] & (query_pos[:, :, None] >= key_pos[:, None, :])
    query_heads = queries.reshape(query_blocks, BLK, HEADS, HD)
    grad_heads = out_grad.reshape(query_blocks, BLK, HEADS, HD)
    raw_scores = (
        jnp.einsum("bqhd,bkhd->bhqk", query_heads, key_tiles, preferred_element_type=jnp.float32)
        * inv_root
    )
    scores = jnp.where(allowed[:, None], raw_scores, -jnp.inf)
    row_max = jnp.max(scores, axis=3)
    log_total = row_max + jnp.log(jnp.sum(jnp.exp(scores - row_max[..., None]), axis=3))
    prob_full = jnp.exp(scores - log_total[..., None])
    prob_low = prob_full.astype(jnp.bfloat16)
    head_output = jnp.einsum(
        "bhqk,bkhd->bqhd", prob_low, value_tiles, preferred_element_type=jnp.float32
    )
    row_delta = jnp.sum(head_output * grad_heads.astype(jnp.float32), axis=3)
    prob_grad = jnp.einsum(
        "bqhd,bkhd->bhqk", grad_heads, value_tiles, preferred_element_type=jnp.float32
    )
    dscore = (prob_full * (prob_grad - jnp.swapaxes(row_delta, 1, 2)[..., None])).astype(
        jnp.bfloat16
    )
    query_total = jnp.einsum(
        "bhqk,bkhd->bqhd", dscore, key_tiles, preferred_element_type=jnp.float32
    )
    query_grad = (query_total * inv_root).reshape(1, local_rows, row_width).astype(jnp.bfloat16)
    key_term = (
        jnp.einsum("bhqk,bqhd->bkhd", dscore, query_heads, preferred_element_type=jnp.float32)
        * inv_root
    )
    value_term = jnp.einsum(
        "bhqk,bqhd->bkhd", prob_low, grad_heads, preferred_element_type=jnp.float32
    )
    flat_lists = lists_here.reshape(query_blocks * NSEL)
    empty_rows = jnp.zeros((block_total, BLK, row_width), jnp.float32)
    key_part = empty_rows.at[flat_lists].add(key_term.reshape(query_blocks * NSEL, BLK, row_width))
    value_part = empty_rows.at[flat_lists].add(
        value_term.reshape(query_blocks * NSEL, BLK, row_width)
    )
    key_sum, value_sum = (
        lax.psum_scatter(
            key_part.reshape(seq_len, row_width).astype(jnp.bfloat16),
            "ctx",
            scatter_dimension=0,
            tiled=True,
        ).astype(jnp.float32),
        lax.psum_scatter(
            value_part.reshape(seq_len, row_width).astype(jnp.bfloat16),
            "ctx",
            scatter_dimension=0,
            tiled=True,
        ).astype(jnp.float32),
    )
    key_grad = key_sum.reshape(1, local_rows, row_width).astype(jnp.bfloat16)
    value_grad = value_sum.reshape(1, local_rows, row_width).astype(jnp.bfloat16)
    tokens_here = expert_input[0]
    grads_here = layer_grad[0]
    expert_count = EXP_DEV * ctx_count
    capacity = min(local_rows, local_rows * TOPK * 4 // (3 * expert_count))
    all_experts = jnp.arange(expert_count, dtype=jnp.int32)
    coef_here = route_coefficients(route_experts[0], route_weight[0], all_experts)
    picked, scaled = slot_rows(tokens_here, grads_here, coef_here, capacity)
    rows_in, grads_in = (
        lax.all_to_all(picked, "ctx", split_axis=0, concat_axis=1, tiled=True),
        lax.all_to_all(scaled, "ctx", split_axis=0, concat_axis=1, tiled=True),
    )
    gate_pre = jnp.einsum("erd,edf->erf", rows_in, gate_weight, preferred_element_type=jnp.float32)
    up_pre = jnp.einsum("erd,edf->erf", rows_in, up_weight, preferred_element_type=jnp.float32)
    gate_sig = jax.nn.sigmoid(gate_pre)
    gate_act = gate_pre * gate_sig
    hidden = (gate_act * up_pre).astype(jnp.bfloat16)
    down_part = jnp.einsum("erd,erf->edf", grads_in, hidden, preferred_element_type=jnp.float32)
    hidden_grad = jnp.einsum(
        "erd,edf->erf", grads_in, down_weight, preferred_element_type=jnp.float32
    )
    gate_delta = (hidden_grad * up_pre * gate_sig * (1.0 + gate_pre * (1.0 - gate_sig))).astype(
        jnp.bfloat16
    )
    up_delta = (hidden_grad * gate_act).astype(jnp.bfloat16)
    gate_part = jnp.einsum("erd,erf->edf", rows_in, gate_delta, preferred_element_type=jnp.float32)
    up_part = jnp.einsum("erd,erf->edf", rows_in, up_delta, preferred_element_type=jnp.float32)
    gate_grad, up_grad, down_grad = (
        lax.psum_scatter(
            gate_part.astype(jnp.bfloat16), "dp", scatter_dimension=1, tiled=True
        ).astype(jnp.float32),
        lax.psum_scatter(
            up_part.astype(jnp.bfloat16), "dp", scatter_dimension=1, tiled=True
        ).astype(jnp.float32),
        lax.psum_scatter(
            down_part.astype(jnp.bfloat16), "dp", scatter_dimension=1, tiled=True
        ).astype(jnp.float32),
    )
    return (query_grad, key_grad, value_grad, gate_grad, up_grad, down_grad)


def solution(mesh):
    in_specs = (
        P("dp", "ctx", None),
        P("dp", "ctx", None),
        P("dp", "ctx", None),
        P("dp", None, None),
        P("dp", None),
        P(),
        P("dp", "ctx", None),
        P("dp", "ctx", None),
        P("dp", "ctx", None),
        P("dp", "ctx", None),
        P("ctx", None, None),
        P("ctx", None, None),
        P("ctx", None, None),
    )
    out_specs = (
        P("dp", "ctx", None),
        P("dp", "ctx", None),
        P("dp", "ctx", None),
        P("ctx", "dp", None),
        P("ctx", "dp", None),
        P("ctx", "dp", None),
    )
    return jax.shard_map(
        per_device, mesh=mesh, in_specs=in_specs, out_specs=out_specs, check_vma=False
    )
```

profile of v0, /device:TPU:2, one launch (start us, length us, event | category | flops | bytes accessed | tf_op | source)
XLA Modules:
  0.0 577.1 jit_solution(10872713448097858192)
XLA Ops:
  10.6 4.2 convolution_convert_fusion
  14.8 6.1 %all-to-all-start = ((bf16[16,64,2048]{2,1,0:T(8,128)(2,1)}), bf16[16,64,2048]{2,1,0:T(8,128)(2,1)}, u32[]{:S(2)}, u32[]{:S(2)}) async-start(bf16[16,64,2048]{2,1,0:T(8,128)(2,1)} %convolution_convert_fusion), calls=%async_computation.2 | async-start | bytes 8388608 | tf_op jit(solution)/shard_map/all_to_all | solution.py:155
  25.3 69.5 %all-to-all-done = bf16[16,64,2048]{2,1,0:T(8,128)(2,1)} async-done(((bf16[16,64,2048]{2,1,0:T(8,128)(2,1)}), bf16[16,64,2048]{2,1,0:T(8,128)(2,1)}, u32[]{:S(2)}, u32[]{:S(2)}) %all-to-all-start) | async-done | bytes 4194336 | tf_op jit(solution)/shard_map/all_to_all | solution.py:155
  94.7 7.8 %all-to-all-start.1 = ((bf16[16,64,2048]{2,1,0:T(8,128)(2,1)}), bf16[16,64,2048]{2,1,0:T(8,128)(2,1)}, u32[]{:S(2)}, u32[]{:S(2)}) async-start(bf16[16,64,2048]{2,1,0:T(8,128)(2,1)} %multiply_convert_fusion), calls=%async_computation.3 | async-start | bytes 8388608 | tf_op jit(solution)/shard_map/all_to_all | solution.py:156
  102.8 7.1 %fusion.3 = f32[1024,704]{0,1:T(8,128)} fusion(bf16[1024,2048]{1,0:T(8,128)(2,1)} %bitcast.33, bf16[1,2048,704]{1,2,0:T(8,128)(2,1)S(1)} %copy-done), kind=kOutput, calls=%fused_computation.13 | convolution fusion | flops 2952790016 | bytes 9961472 | tf_op jit(solution)/shard_map/erd,edf->erf/dot_general | solution.py:158
  109.9 7.1 %fusion.5 = f32[1024,704]{0,1:T(8,128)} fusion(bf16[1024,2048]{1,0:T(8,128)(2,1)} %bitcast.33, bf16[1,2048,704]{1,2,0:T(8,128)(2,1)S(1)} %copy-done.8), kind=kOutput, calls=%fused_computation.15 | convolution fusion | flops 2952790016 | bytes 9961472 | tf_op jit(solution)/shard_map/erd,edf->erf/dot_general | solution.py:159
  117.1 45.9 %all-to-all-done.1 = bf16[16,64,2048]{2,1,0:T(8,128)(2,1)} async-done(((bf16[16,64,2048]{2,1,0:T(8,128)(2,1)}), bf16[16,64,2048]{2,1,0:T(8,128)(2,1)}, u32[]{:S(2)}, u32[]{:S(2)}) %all-to-all-start.1) | async-done | bytes 4194336 | tf_op jit(solution)/shard_map/all_to_all | solution.py:156
  163.0 5.2 fusion.7
  169.7 7.4 %fusion = bf16[1,2048,704]{1,2,0:T(8,128)(2,1)} fusion(bf16[1024,2048]{1,0:T(8,128)(2,1)} %bitcast.33, f32[1024,704]{0,1:T(8,128)S(1)} %copy-done.10, f32[1024,704]{0,1:T(8,128)S(1)} %fusion.7, f32[1024,704]{0,1:T(8,128)S(1)} %copy-done.12), kind=kOutput, calls=%fused_computation.10 | convolution fusion | flops 2961440768 | bytes 15728640 | tf_op jit(solution)/shard_map/erd,erf->edf/dot_general | solution.py:171
  179.0 7.9 %fusion.1 = bf16[1,2048,704]{1,2,0:T(8,128)(2,1)} fusion(bf16[1024,2048]{1,0:T(8,128)(2,1)} %bitcast.33, f32[1024,704]{0,1:T(8,128)} %copy-done.13, f32[1024,704]{0,1:T(8,128)S(1)} %copy-done.11), kind=kOutput, calls=%fused_computation.11 | convolution fusion | flops 2958557184 | bytes 12845056 | tf_op jit(solution)/shard_map/erd,erf->edf/dot_general | solution.py:172
  187.0 7.9 %fusion.2 = bf16[1,2048,704]{1,2,0:T(8,128)(2,1)} fusion(bf16[1024,2048]{1,0:T(8,128)(2,1)} %bitcast.35, f32[1024,704]{0,1:T(8,128)} %fusion.5, f32[1024,704]{0,1:T(8,128)S(1)} %copy-done.11), kind=kOutput, calls=%fused_computation.12 | convolution fusion | flops 2958557184 | bytes 12845056 | tf_op jit(solution)/shard_map/erd,erf->edf/dot_general | solution.py:163
  195.3 3.9 convolution_convert_fusion.4
  201.1 5.3 copy.93
  211.0 5.4 copy.95
  231.1 4.3 broadcast_in_dim.38.clone
  235.5 4.5 scatter_fusion
  240.0 6.1 %convert_element_type.125 = bf16[16,128,1024]{2,1,0:T(8,128)(2,1)} convert(f32[16,128,1024]{2,1,0:T(8,128)} %scatter_fusion) | non-fusion elementwise | flops 2097152 | bytes 12582912 | tf_op jit(solution)/shard_map/convert_element_type | solution.py:133
  253.0 4.4 broadcast_in_dim.38.clone.1
  257.4 4.1 scatter_fusion.1
  261.5 6.1 %convert_element_type.128 = bf16[16,128,1024]{2,1,0:T(8,128)(2,1)} convert(f32[16,128,1024]{2,1,0:T(8,128)} %scatter_fusion.1) | non-fusion elementwise | flops 2097152 | bytes 12582912 | tf_op jit(solution)/shard_map/convert_element_type | solution.py:139
  272.5 75.3 %reduce-scatter.12.cloned.1.call-done = bf16[1,256,704]{1,2,0:T(8,128)(2,1)} async-done(((bf16[1,2048,704]{1,2,0:T(8,128)(2,1)}), bf16[1,256,704]{1,2,0:T(8,128)(2,1)}) %reduce-scatter.12.cloned.1.call-update) | async-done | bytes 360464 | tf_op jit(solution)/shard_map/reduce_scatter | solution.py:177
  349.7 79.9 %reduce-scatter.14.cloned.1.call-done = bf16[1,256,704]{1,2,0:T(8,128)(2,1)} async-done(((bf16[1,2048,704]{1,2,0:T(8,128)(2,1)}), bf16[1,256,704]{1,2,0:T(8,128)(2,1)}) %reduce-scatter.14.cloned.1.call-update) | async-done | bytes 360464 | tf_op jit(solution)/shard_map/reduce_scatter | solution.py:180
  431.5 68.1 %reduce-scatter.6.cloned.1.call-done = bf16[128,1024]{1,0:T(8,128)(2,1)} async-done(((bf16[2048,1024]{1,0:T(8,128)(2,1)}), bf16[128,1024]{1,0:T(8,128)(2,1)}) %reduce-scatter.6.cloned.1.call-update) | async-done | bytes 262160 | tf_op jit(solution)/shard_map/reduce_scatter | solution.py:132
  499.6 69.9 %reduce-scatter.8.cloned.1.call-done = bf16[128,1024]{1,0:T(8,128)(2,1)} async-done(((bf16[2048,1024]{1,0:T(8,128)(2,1)}), bf16[128,1024]{1,0:T(8,128)(2,1)}) %reduce-scatter.8.cloned.1.call-update) | async-done | bytes 262160 | tf_op jit(solution)/shard_map/reduce_scatter | solution.py:138
  (93 shorter events, 47.4 us)
Async XLA Ops:
  8.0 94.8 %copy-start = (bf16[1,2048,704]{1,2,0:T(8,128)(2,1)S(1)}, bf16[1,2048,704]{1,2,0:T(8,128)(2,1)}, u32[]{:S(2)}) copy-start(bf16[1,2048,704]{1,2,0:T(8,128)(2,1)} %param.23) | copy-start | bytes 8650756
  8.0 193.1 %all-gather.5.cloned.1.call-start = ((), (), s32[]{:S(2)}) async-start(), calls=%async_computation.12 | async-start | bytes 4456448 | tf_op jit(solution)/shard_map/all_gather | solution.py:63
  14.8 7.1 %copy-start.5 = (bf16[1,128,2048]{2,1,0:T(8,128)(2,1)S(1)}, bf16[1,128,2048]{2,1,0:T(8,128)(2,1)}, u32[]{:S(2)}) copy-start(bf16[1,128,2048]{2,1,0:T(8,128)(2,1)} %param.20) | copy-start | bytes 1572868
  14.8 79.9 %all-to-all-start = ((bf16[16,64,2048]{2,1,0:T(8,128)(2,1)}), bf16[16,64,2048]{2,1,0:T(8,128)(2,1)}, u32[]{:S(2)}, u32[]{:S(2)}) async-start(bf16[16,64,2048]{2,1,0:T(8,128)(2,1)} %convolution_convert_fusion), calls=%async_computation.2 | async-start | bytes 8388608 | tf_op jit(solution)/shard_map/all_to_all | solution.py:155
  21.0 190.0 %all-gather.7.cloned.1.call-start = ((), (), s32[]{:S(2)}) async-start(), calls=%async_computation.13 | async-start | bytes 4456448 | tf_op jit(solution)/shard_map/all_gather | solution.py:64
  94.7 68.3 %all-to-all-start.1 = ((bf16[16,64,2048]{2,1,0:T(8,128)(2,1)}), bf16[16,64,2048]{2,1,0:T(8,128)(2,1)}, u32[]{:S(2)}, u32[]{:S(2)}) async-start(bf16[16,64,2048]{2,1,0:T(8,128)(2,1)} %multiply_convert_fusion), calls=%async_computation.3 | async-start | bytes 8388608 | tf_op jit(solution)/shard_map/all_to_all | solution.py:156
  102.6 168.0 %reduce-scatter.10.cloned.1.call-start = ((), (), s32[]{:S(2)}) async-start(), calls=%async_computation.9 | async-start | bytes 3244032 | tf_op jit(solution)/shard_map/reduce_scatter | solution.py:174
  102.8 7.1 %copy-start.8 = (bf16[1,2048,704]{1,2,0:T(8,128)(2,1)S(1)}, bf16[1,2048,704]{1,2,0:T(8,128)(2,1)}, u32[]{:S(2)}) copy-start(bf16[1,2048,704]{1,2,0:T(8,128)(2,1)} %param.24) | copy-start | bytes 8650756
  109.9 53.1 %copy-start.9 = (bf16[1,2048,704]{1,2,0:T(8,128)(2,1)S(1)}, bf16[1,2048,704]{1,2,0:T(8,128)(2,1)}, u32[]{:S(2)}) copy-start(bf16[1,2048,704]{1,2,0:T(8,128)(2,1)} %param.25) | copy-start | bytes 8650756
  163.0 6.7 %copy-start.10 = (f32[1024,704]{0,1:T(8,128)S(1)}, f32[1024,704]{0,1:T(8,128)}, u32[]{:S(2)}) copy-start(f32[1024,704]{0,1:T(8,128)} %fusion.3) | copy-start | bytes 8650756
  163.0 6.7 %copy-start.12 = (f32[1024,704]{0,1:T(8,128)S(1)}, f32[1024,704]{0,1:T(8,128)}, u32[]{:S(2)}) copy-start(f32[1024,704]{0,1:T(8,128)} %fusion.5) | copy-start | bytes 8650756
  168.2 1.5 copy-start.13
  177.1 1.9 copy-start.11
  177.2 170.6 %reduce-scatter.12.cloned.1.call-start = ((), (), s32[]{:S(2)}) async-start(), calls=%async_computation.10 | async-start | bytes 3244032 | tf_op jit(solution)/shard_map/reduce_scatter | solution.py:177
  187.0 242.6 %reduce-scatter.14.cloned.1.call-start = ((), (), s32[]{:S(2)}) async-start(), calls=%async_computation.11 | async-start | bytes 3244032 | tf_op jit(solution)/shard_map/reduce_scatter | solution.py:180
  194.9 304.6 %reduce-scatter.6.cloned.1.call-start = ((), (), s32[]{:S(2)}) async-start(), calls=%async_computation.7 | async-start | bytes 4456448 | tf_op jit(solution)/shard_map/reduce_scatter | solution.py:132
  195.2 4.3 copy-start.6
  195.2 4.4 copy-start.7
  195.2 4.8 copy-start.2
  220.9 2.2 copy-start.3
  224.4 1.0 copy-start.4
  246.1 323.4 %reduce-scatter.8.cloned.1.call-start = ((), (), s32[]{:S(2)}) async-start(), calls=%async_computation.8 | async-start | bytes 4456448 | tf_op jit(solution)/shard_map/reduce_scatter | solution.py:138
  267.6 301.9 %copy-start.1 = (bf16[1,2048,704]{1,2,0:T(8,128)(2,1)S(1)}, bf16[1,2048,704]{1,2,0:T(8,128)(2,1)}, u32[]{:S(2)}) copy-start(bf16[1,2048,704]{1,2,0:T(8,128)(2,1)} %param.23) | copy-start | bytes 8650756
Sparse Core Ops, SparseCore 0:
  10.5 81.0 all-gather.4
  93.3 89.8 all-gather.6
Sparse Core Ops, SparseCore 1:
  177.2 88.6 reduce-scatter.9
  269.6 78.1 reduce-scatter.11
  351.5 78.0 reduce-scatter.13
  432.6 67.0 reduce-scatter.5
  502.6 66.9 reduce-scatter.7
where the time goes:
time: 578 us; the launch traced here: 577 us
  waiting for transfers between devices  410 us (71%)
  matrix products  61.6 us (11%)
  local copies, waits for them, and re-layouts  46.8 us (8%)
  other arithmetic  27.7 us (5%)
  between operations  16 us (3%)
  starting transfers between devices  14.9 us (3%)
    reduce_scatter x1, waiting for transfers between devices, per_device(): lax.psum_scatter(down_part.astype(jnp.bfloat16), 'dp', scatter_dimension=...  79.9 us
    reduce_scatter x1, waiting for transfers between devices, per_device(): lax.psum_scatter(up_part.astype(jnp.bfloat16), 'dp', scatter_dimension=1,...  75.3 us
    reduce_scatter x1, waiting for transfers between devices, per_device(): lax.psum_scatter(value_part.reshape(seq_len, row_width).astype(jnp.bfloat...  69.9 us
    all_to_all x1, waiting for transfers between devices, per_device(): lax.all_to_all(picked, 'ctx', split_axis=0, concat_axis=1, tiled=True)  69.5 us
    reduce_scatter x1, waiting for transfers between devices, per_device(): lax.psum_scatter(key_part.reshape(seq_len, row_width).astype(jnp.bfloat16...  68.1 us
    all_to_all x1, waiting for transfers between devices, per_device(): lax.all_to_all(scaled, 'ctx', split_axis=0, concat_axis=1, tiled=True)  45.9 us
    unnamed x34, local copies, waits for them, and re-layouts  17.5 us
  transfers between devices with their start and end apart: 9, of which 6 were waited for; matrix products, arithmetic and copies ran while one was open for 23% of the time, Pallas kernels for 0%

commit v1 on v0

--- a/solution.py
+++ b/solution.py
@@ -152,7 +152,10 @@
     coef_here = route_coefficients(route_experts[0], route_weight[0], all_experts)
     picked, scaled = slot_rows(tokens_here, grads_here, coef_here, capacity)
     rows_in, grads_in = (
-        lax.all_to_all(picked, "ctx", split_axis=0, concat_axis=1, tiled=True),
+        jnp.concatenate(
+            lax.all_to_all(jnp.stack(jnp.split(picked, lax.axis_size("ctx"), axis=0)), "ctx", 0, 0),
+            axis=1,
+        ),
         lax.all_to_all(scaled, "ctx", split_axis=0, concat_axis=1, tiled=True),
     )
     gate_pre = jnp.einsum("erd,edf->erf", rows_in, gate_weight, preferred_element_type=jnp.float32)

time: 578 us -> 588 us (1.017)
  local copies, waits for them, and re-layouts: 46.8 us -> 56.6 us
    unnamed x34 -> x49, local copies, waits for them, and re-layouts: 17.5 us -> 26.5 us
    all_to_all x1, waiting for transfers between devices: 45.9 us -> 53.8 us  [per_device(): lax.all_to_all(scaled, 'ctx', split_axis=0, concat_axis=1, tiled=True)]
    all_to_all x1, waiting for transfers between devices: 69.5 us -> 61.8 us  [per_device(): lax.all_to_all(jnp.stack(jnp.split(picked, lax.axis_size('ctx'), axis=0))...]
  transfers between devices with their start and end apart: 9 -> 9, of which waited for: 6 -> 6; matrix products, arithmetic and copies ran while one was open for 23% -> 24% of each run, Pallas kernels for 0% -> 0%
where the time goes in v1:
time: 588 us; the launch traced here: 587 us
  waiting for transfers between devices  410 us (70%)
  matrix products  59.4 us (10%)
  local copies, waits for them, and re-layouts  56.6 us (10%)
  other arithmetic  27.4 us (5%)
  starting transfers between devices  18.2 us (3%)
  between operations  16 us (3%)
    reduce_scatter x1, waiting for transfers between devices, per_device(): lax.psum_scatter(down_part.astype(jnp.bfloat16), 'dp', scatter_dimension=...  79.9 us
    reduce_scatter x1, waiting for transfers between devices, per_device(): lax.psum_scatter(up_part.astype(jnp.bfloat16), 'dp', scatter_dimension=1,...  74.9 us
    reduce_scatter x1, waiting for transfers between devices, per_device(): lax.psum_scatter(value_part.reshape(seq_len, row_width).astype(jnp.bfloat...  69.8 us
    reduce_scatter x1, waiting for transfers between devices, per_device(): lax.psum_scatter(key_part.reshape(seq_len, row_width).astype(jnp.bfloat16...  68 us
    all_to_all x1, waiting for transfers between devices, per_device(): lax.all_to_all(jnp.stack(jnp.split(picked, lax.axis_size('ctx'), axis=0))...  61.8 us
    all_to_all x1, waiting for transfers between devices, per_device(): lax.all_to_all(scaled, 'ctx', split_axis=0, concat_axis=1, tiled=True)  53.8 us
    unnamed x49, local copies, waits for them, and re-layouts  26.5 us
  transfers between devices with their start and end apart: 9, of which 6 were waited for; matrix products, arithmetic and copies ran while one was open for 24% of the time, Pallas kernels for 0%

profile of v1, /device:TPU:2, one launch (start us, length us, event | category | flops | bytes accessed | tf_op | source)
XLA Modules:
  0.0 587.4 jit_solution(1197341654157299679)
XLA Ops:
  24.5 6.1 %all-to-all-start = ((bf16[16,1,64,2048]{3,2,1,0:T(8,128)(2,1)}), bf16[16,1,64,2048]{3,2,1,0:T(8,128)(2,1)}, u32[]{:S(2)}, u32[]{:S(2)}) async-start(bf16[16,1,64,2048]{3,2,1,0:T(8,128)(2,1)} %fusion.25), calls=%async_computation.2 | async-start | bytes 8388608 | tf_op jit(solution)/shard_map/all_to_all | solution.py:156
  31.6 3.2 multiply_convert_fusion
  34.8 61.8 %all-to-all-done = bf16[16,1,64,2048]{3,2,1,0:T(8,128)(2,1)} async-done(((bf16[16,1,64,2048]{3,2,1,0:T(8,128)(2,1)}), bf16[16,1,64,2048]{3,2,1,0:T(8,128)(2,1)}, u32[]{:S(2)}, u32[]{:S(2)}) %all-to-all-start) | async-done | bytes 4194336 | tf_op jit(solution)/shard_map/all_to_all | solution.py:156
  96.6 11.1 %all-to-all-start.1 = ((bf16[16,64,2048]{2,1,0:T(8,128)(2,1)}), bf16[16,64,2048]{2,1,0:T(8,128)(2,1)}, u32[]{:S(2)}, u32[]{:S(2)}) async-start(bf16[16,64,2048]{2,1,0:T(8,128)(2,1)} %multiply_convert_fusion), calls=%async_computation.3 | async-start | bytes 8388608 | tf_op jit(solution)/shard_map/all_to_all | solution.py:159
  108.0 7.1 %fusion.3 = f32[1024,704]{0,1:T(8,128)} fusion(bf16[1024,2048]{1,0:T(8,128)(2,1)} %bitcast.49, bf16[1,2048,704]{1,2,0:T(8,128)(2,1)S(1)} %copy-done), kind=kOutput, calls=%fused_computation.13 | convolution fusion | flops 2952790016 | bytes 9961472 | tf_op jit(solution)/shard_map/erd,edf->erf/dot_general | solution.py:161
  115.1 7.2 %fusion.5 = f32[1024,704]{0,1:T(8,128)} fusion(bf16[1024,2048]{1,0:T(8,128)(2,1)} %bitcast.49, bf16[1,2048,704]{1,2,0:T(8,128)(2,1)S(1)} %copy-done.8), kind=kOutput, calls=%fused_computation.15 | convolution fusion | flops 2952790016 | bytes 9961472 | tf_op jit(solution)/shard_map/erd,edf->erf/dot_general | solution.py:162
  122.4 53.8 %all-to-all-done.1 = bf16[16,64,2048]{2,1,0:T(8,128)(2,1)} async-done(((bf16[16,64,2048]{2,1,0:T(8,128)(2,1)}), bf16[16,64,2048]{2,1,0:T(8,128)(2,1)}, u32[]{:S(2)}, u32[]{:S(2)}) %all-to-all-start.1) | async-done | bytes 4194336 | tf_op jit(solution)/shard_map/all_to_all | solution.py:159
  176.1 5.1 fusion.7
  183.0 7.5 %fusion = bf16[1,2048,704]{1,2,0:T(8,128)(2,1)} fusion(bf16[1024,2048]{1,0:T(8,128)(2,1)} %bitcast.49, f32[1024,704]{0,1:T(8,128)S(1)} %copy-done.10, f32[1024,704]{0,1:T(8,128)S(1)} %fusion.7, f32[1024,704]{0,1:T(8,128)S(1)} %copy-done.12), kind=kOutput, calls=%fused_computation.10 | convolution fusion | flops 2961440768 | bytes 15728640 | tf_op jit(solution)/shard_map/erd,erf->edf/dot_general | solution.py:174
  190.6 7.9 %fusion.1 = bf16[1,2048,704]{1,2,0:T(8,128)(2,1)} fusion(bf16[1024,2048]{1,0:T(8,128)(2,1)} %bitcast.49, f32[1024,704]{0,1:T(8,128)} %copy-done.13, f32[1024,704]{0,1:T(8,128)S(1)} %copy-done.11), kind=kOutput, calls=%fused_computation.11 | convolution fusion | flops 2958557184 | bytes 12845056 | tf_op jit(solution)/shard_map/erd,erf->edf/dot_general | solution.py:175
  198.5 7.8 %fusion.2 = bf16[1,2048,704]{1,2,0:T(8,128)(2,1)} fusion(bf16[1024,2048]{1,0:T(8,128)(2,1)} %bitcast.51, f32[1024,704]{0,1:T(8,128)} %fusion.5, f32[1024,704]{0,1:T(8,128)S(1)} %copy-done.11), kind=kOutput, calls=%fused_computation.12 | convolution fusion | flops 2958557184 | bytes 12845056 | tf_op jit(solution)/shard_map/erd,erf->edf/dot_general | solution.py:166
  206.7 3.7 convolution_convert_fusion.4
  212.3 5.3 copy.93
  222.2 5.3 copy.95
  242.2 4.3 broadcast_in_dim.38.clone
  246.5 4.5 scatter_fusion
  251.0 6.0 %convert_element_type.125 = bf16[16,128,1024]{2,1,0:T(8,128)(2,1)} convert(f32[16,128,1024]{2,1,0:T(8,128)} %scatter_fusion) | non-fusion elementwise | flops 2097152 | bytes 12582912 | tf_op jit(solution)/shard_map/convert_element_type | solution.py:133
  264.2 4.3 broadcast_in_dim.38.clone.1
  268.5 3.9 scatter_fusion.1
  272.4 6.0 %convert_element_type.128 = bf16[16,128,1024]{2,1,0:T(8,128)(2,1)} convert(f32[16,128,1024]{2,1,0:T(8,128)} %scatter_fusion.1) | non-fusion elementwise | flops 2097152 | bytes 12582912 | tf_op jit(solution)/shard_map/convert_element_type | solution.py:139
  283.3 74.9 %reduce-scatter.12.cloned.1.call-done = bf16[1,256,704]{1,2,0:T(8,128)(2,1)} async-done(((bf16[1,2048,704]{1,2,0:T(8,128)(2,1)}), bf16[1,256,704]{1,2,0:T(8,128)(2,1)}) %reduce-scatter.12.cloned.1.call-update) | async-done | bytes 360464 | tf_op jit(solution)/shard_map/reduce_scatter | solution.py:180
  360.1 79.9 %reduce-scatter.14.cloned.1.call-done = bf16[1,256,704]{1,2,0:T(8,128)(2,1)} async-done(((bf16[1,2048,704]{1,2,0:T(8,128)(2,1)}), bf16[1,256,704]{1,2,0:T(8,128)(2,1)}) %reduce-scatter.14.cloned.1.call-update) | async-done | bytes 360464 | tf_op jit(solution)/shard_map/reduce_scatter | solution.py:183
  441.9 68.0 %reduce-scatter.6.cloned.1.call-done = bf16[128,1024]{1,0:T(8,128)(2,1)} async-done(((bf16[2048,1024]{1,0:T(8,128)(2,1)}), bf16[128,1024]{1,0:T(8,128)(2,1)}) %reduce-scatter.6.cloned.1.call-update) | async-done | bytes 262160 | tf_op jit(solution)/shard_map/reduce_scatter | solution.py:132
  510.0 69.8 %reduce-scatter.8.cloned.1.call-done = bf16[128,1024]{1,0:T(8,128)(2,1)} async-done(((bf16[2048,1024]{1,0:T(8,128)(2,1)}), bf16[128,1024]{1,0:T(8,128)(2,1)}) %reduce-scatter.8.cloned.1.call-update) | async-done | bytes 262160 | tf_op jit(solution)/shard_map/reduce_scatter | solution.py:138
  (109 shorter events, 56.6 us)
Async XLA Ops:
  8.0 100.0 %copy-start = (bf16[1,2048,704]{1,2,0:T(8,128)(2,1)S(1)}, bf16[1,2048,704]{1,2,0:T(8,128)(2,1)}, u32[]{:S(2)}) copy-start(bf16[1,2048,704]{1,2,0:T(8,128)(2,1)} %param.23) | copy-start | bytes 8650756
  8.0 204.3 %all-gather.5.cloned.1.call-start = ((), (), s32[]{:S(2)}) async-start(), calls=%async_computation.12 | async-start | bytes 4456448 | tf_op jit(solution)/shard_map/all_gather | solution.py:63
  24.5 7.1 %copy-start.5 = (bf16[1,128,2048]{2,1,0:T(8,128)(2,1)S(1)}, bf16[1,128,2048]{2,1,0:T(8,128)(2,1)}, u32[]{:S(2)}) copy-start(bf16[1,128,2048]{2,1,0:T(8,128)(2,1)} %param.20) | copy-start | bytes 1572868
  24.5 72.1 %all-to-all-start = ((bf16[16,1,64,2048]{3,2,1,0:T(8,128)(2,1)}), bf16[16,1,64,2048]{3,2,1,0:T(8,128)(2,1)}, u32[]{:S(2)}, u32[]{:S(2)}) async-start(bf16[16,1,64,2048]{3,2,1,0:T(8,128)(2,1)} %fusion.25), calls=%async_computation.2 | async-start | bytes 8388608 | tf_op jit(solution)/shard_map/all_to_all | solution.py:156
  30.6 191.6 %all-gather.7.cloned.1.call-start = ((), (), s32[]{:S(2)}) async-start(), calls=%async_computation.13 | async-start | bytes 4456448 | tf_op jit(solution)/shard_map/all_gather | solution.py:64
  96.6 79.5 %all-to-all-start.1 = ((bf16[16,64,2048]{2,1,0:T(8,128)(2,1)}), bf16[16,64,2048]{2,1,0:T(8,128)(2,1)}, u32[]{:S(2)}, u32[]{:S(2)}) async-start(bf16[16,64,2048]{2,1,0:T(8,128)(2,1)} %multiply_convert_fusion), calls=%async_computation.3 | async-start | bytes 8388608 | tf_op jit(solution)/shard_map/all_to_all | solution.py:159
  107.8 173.7 %reduce-scatter.10.cloned.1.call-start = ((), (), s32[]{:S(2)}) async-start(), calls=%async_computation.9 | async-start | bytes 3244032 | tf_op jit(solution)/shard_map/reduce_scatter | solution.py:177
  108.0 7.1 %copy-start.8 = (bf16[1,2048,704]{1,2,0:T(8,128)(2,1)S(1)}, bf16[1,2048,704]{1,2,0:T(8,128)(2,1)}, u32[]{:S(2)}) copy-start(bf16[1,2048,704]{1,2,0:T(8,128)(2,1)} %param.24) | copy-start | bytes 8650756
  115.1 61.0 %copy-start.9 = (bf16[1,2048,704]{1,2,0:T(8,128)(2,1)S(1)}, bf16[1,2048,704]{1,2,0:T(8,128)(2,1)}, u32[]{:S(2)}) copy-start(bf16[1,2048,704]{1,2,0:T(8,128)(2,1)} %param.25) | copy-start | bytes 8650756
  176.1 6.8 %copy-start.10 = (f32[1024,704]{0,1:T(8,128)S(1)}, f32[1024,704]{0,1:T(8,128)}, u32[]{:S(2)}) copy-start(f32[1024,704]{0,1:T(8,128)} %fusion.3) | copy-start | bytes 8650756
  176.1 6.8 %copy-start.12 = (f32[1024,704]{0,1:T(8,128)S(1)}, f32[1024,704]{0,1:T(8,128)}, u32[]{:S(2)}) copy-start(f32[1024,704]{0,1:T(8,128)} %fusion.5) | copy-start | bytes 8650756
  181.3 1.7 copy-start.13
  183.0 7.6 %copy-start.11 = (f32[1024,704]{0,1:T(8,128)S(1)}, f32[1024,704]{0,1:T(8,128)}, u32[]{:S(2)}) copy-start(f32[1024,704]{0,1:T(8,128)} %fusion.3) | copy-start | bytes 8650756
  190.5 167.7 %reduce-scatter.12.cloned.1.call-start = ((), (), s32[]{:S(2)}) async-start(), calls=%async_computation.10 | async-start | bytes 3244032 | tf_op jit(solution)/shard_map/reduce_scatter | solution.py:180
  198.5 241.5 %reduce-scatter.14.cloned.1.call-start = ((), (), s32[]{:S(2)}) async-start(), calls=%async_computation.11 | async-start | bytes 3244032 | tf_op jit(solution)/shard_map/reduce_scatter | solution.py:183
  206.4 4.4 copy-start.6
  206.4 4.4 copy-start.7
  206.4 4.8 copy-start.2
  206.4 303.6 %reduce-scatter.6.cloned.1.call-start = ((), (), s32[]{:S(2)}) async-start(), calls=%async_computation.7 | async-start | bytes 4456448 | tf_op jit(solution)/shard_map/reduce_scatter | solution.py:132
  232.0 2.2 copy-start.3
  235.5 1.0 copy-start.4
  257.1 322.7 %reduce-scatter.8.cloned.1.call-start = ((), (), s32[]{:S(2)}) async-start(), calls=%async_computation.8 | async-start | bytes 4456448 | tf_op jit(solution)/shard_map/reduce_scatter | solution.py:138
  278.4 301.4 %copy-start.1 = (bf16[1,2048,704]{1,2,0:T(8,128)(2,1)S(1)}, bf16[1,2048,704]{1,2,0:T(8,128)(2,1)}, u32[]{:S(2)}) copy-start(bf16[1,2048,704]{1,2,0:T(8,128)(2,1)} %param.23) | copy-start | bytes 8650756
Sparse Core Ops, SparseCore 0:
  10.5 81.3 all-gather.4
  93.6 77.9 all-gather.6
Sparse Core Ops, SparseCore 1:
  190.6 85.7 reduce-scatter.9
  280.1 78.0 reduce-scatter.11
  361.9 78.0 reduce-scatter.13
  443.0 66.9 reduce-scatter.5
  513.0 66.8 reduce-scatter.7
